TPU v7x, 32 devices: a whole 2x2x4 slice. The times are simulated.
32 devices in a mesh: row: 4 (over z), col: 8 (over y, x, core).
Axes of the slice: x: 2, y: 2, z: 4, core: 2. Of those that a mesh axis runs over, the one named last changes fastest.
Arguments:
- factor_panel: bfloat16 [1024, 8192], P('row', 'col'), may hold values from -0.1875 to 0.1875
- ancestor_inv: float32 [1024, 1024], P('row', 'col'), may hold values from -6 to 6
- diag_inverse: float32 [4096, 8192], P('row', 'col'), may hold values from -6 to 6
- structure: int32 [2, 4], replicated, may hold values 0 or 1
Outputs:
- inverse_panel: float32 [1024, 8192], P('row', 'col')
- diag_sigma: float32 [4096, 8192], P('row', 'col')
All inputs are finite; a program needn't handle non-finite values.
Results may differ from a plain program's by a relative error of at most 0.0003.
Values may be sent and summed in bfloat16 or wider, within the bound.
A program may use at most 128 MiB of HBM per device.

v0:
```python
import jax
import jax.numpy as jnp
from jax import lax
from jax.sharding import PartitionSpec as P

B = 256
NS = 2


def local(factor_panel, ancestor_inv, diag_inverse, structure):
    rows_dev, width_dev = factor_panel.shape
    per_block = width_dev // NS
    row_index = lax.axis_index("row")
    keep_tiles = jnp.repeat(structure, B, axis=1)
    keep_own = lax.dynamic_slice_in_dim(keep_tiles, row_index * rows_dev, rows_dev, 1)
    keep_cols = jnp.repeat(keep_own.T, per_block, axis=1)
    lhat_local = jnp.where(keep_cols == 1, factor_panel, jnp.zeros_like(factor_panel))
    column = lax.all_gather(lhat_local, "row", axis=0, tiled=True)
    sigma_rows = lax.all_gather(ancestor_inv, "col", axis=1, tiled=True)
    column_wide = column.astype(jnp.float32)
    running = jnp.dot(sigma_rows, column_wide, precision=lax.Precision.HIGHEST)
    inverse_panel = jnp.where(keep_cols == 1, -running, jnp.zeros_like(running))
    rows_all = lax.all_gather(lhat_local, "col", axis=1, tiled=True)
    block_count = rows_all.shape[1] // width_dev
    rows_cube = rows_all.reshape(rows_dev, block_count, NS, per_block)
    lhat_members = [
        rows_cube[:, :, member, :].reshape(rows_dev, block_count * per_block).astype(jnp.float32)
        for member in range(NS)
    ]
    pieces = []
    for member in range(NS):
        window = lhat_members[member]
        target = inverse_panel[:, member * per_block : (member + 1) * per_block]
        pieces.append(
            lax.dot_general(
                window,
                target,
                (((0,), (0,)), ((), ())),
                precision=lax.Precision.HIGHEST,
                preferred_element_type=jnp.float32,
            )
        )
    update = lax.psum_scatter(
        jnp.concatenate(pieces, axis=1), "row", scatter_dimension=0, tiled=True
    )
    diag_sigma = diag_inverse - update
    return (inverse_panel, diag_sigma)


def solution(mesh):
    placed = (P("row", "col"), P("row", "col"), P("row", "col"), P())
    return jax.shard_map(
        local,
        mesh=mesh,
        in_specs=placed,
        out_specs=(P("row", "col"), P("row", "col")),
        check_vma=False,
    )
```

profile of v0, /device:TPU:5, one launch (start us, length us, event | category | flops | bytes accessed | tf_op | source)
XLA Modules:
  0.0 435.5 jit_solution(3430236630493984573)
XLA Ops:
  7.2 0.0 copy-start
  7.2 0.0 all-gather.6.cloned.1.call-start
  7.2 0.7 all-gather.6.cloned.1.call-update
  7.9 0.0 all-gather.4.cloned.1.call-start
  8.0 0.0 copy-done
  8.0 0.1 broadcast_bitcast_fusion
  8.1 1.2 copy.6
  9.3 0.8 bitcast_select_fusion.1
  10.2 0.0 all-gather.4.cloned.1.call-update
  10.2 0.0 all-gather.8.cloned.1.call-start
  10.2 0.7 all-gather.8.cloned.1.call-update
  10.9 0.0 reduce-scatter.2.cloned.1.call-start
  11.0 24.0 %all-gather.6.cloned.1.call-done = f32[256,1024]{1,0:T(8,128)} async-done(((f32[256,128]{1,0:T(8,128)}), f32[256,1024]{1,0:T(8,128)}) %all-gather.6.cloned.1.call-update) | async-done | bytes 1048592 | tf_op jit(solution)/shard_map/all_gather | solution.py:19
  35.0 48.4 %all-gather.4.cloned.1.call-done = bf16[1024,1024]{0,1:T(8,128)(2,1)} async-done(((bf16[256,1024]{0,1:T(8,128)(2,1)}), bf16[1024,1024]{0,1:T(8,128)(2,1)}) %all-gather.4.cloned.1.call-update) | async-done | bytes 2097168 | tf_op jit(solution)/shard_map/all_gather | solution.py:18
  83.4 3.7 bitcast_select_fusion
  87.1 33.7 %all-gather.8.cloned.1.call-done = bf16[256,8192]{0,1:T(8,128)(2,1)} async-done(((bf16[256,1024]{0,1:T(8,128)(2,1)}), bf16[256,8192]{0,1:T(8,128)(2,1)}) %all-gather.8.cloned.1.call-update) | async-done | bytes 4194320 | tf_op jit(solution)/shard_map/all_gather | solution.py:23
  120.8 2.6 fusion.5
  123.4 3.5 fusion.1
  126.9 3.5 fusion.3
  130.3 6.4 %pad_maximum_fusion = f32[4096,1024]{0,1:T(8,128)} fusion(f32[4096,512]{0,1:T(8,128)S(1)} %fusion.1, f32[4096,512]{0,1:T(8,128)S(1)} %fusion.3), kind=kLoop, calls=%fused_computation | loop fusion | flops 4194304 | bytes 33554432 | tf_op jit(solution)/shard_map/concatenate | solution.py:44
  136.7 0.0 reduce-scatter.2.cloned.1.call-update
  136.7 5.3 %copy.7 = f32[1024,1024]{0,1:T(8,128)} copy(f32[1024,1024]{1,0:T(8,128)} %param.6) | data formatting | bytes 8388608 | tf_op args[2]
  142.1 1.3 copy.8
  143.4 273.4 %reduce-scatter.2.cloned.1.call-done = f32[1024,1024]{0,1:T(8,128)} async-done(((f32[4096,1024]{0,1:T(8,128)}), f32[1024,1024]{0,1:T(8,128)}) %reduce-scatter.2.cloned.1.call-update) | async-done | bytes 4194320 | tf_op jit(solution)/shard_map/reduce_scatter | solution.py:43
  416.8 0.0 copy-start.1
  416.8 6.8 %sub.3 = f32[1024,1024]{0,1:T(8,128)} subtract(f32[1024,1024]{0,1:T(8,128)} %copy.7, f32[1024,1024]{0,1:T(8,128)} %reduce-scatter.2.cloned.1.call-done) | non-fusion elementwise | flops 1048576 | bytes 12582912 | tf_op jit(solution)/shard_map/sub | solution.py:46
  423.6 5.3 %copy.9 = f32[1024,1024]{1,0:T(8,128)} copy(f32[1024,1024]{0,1:T(8,128)} %sub.3) | data formatting | bytes 8388608
  428.9 0.0 copy-done.1
  (2 shorter events, 0.0 us)
Async XLA Ops:
  7.2 0.8 copy-start
  7.2 27.8 %all-gather.6.cloned.1.call-start = ((), (), s32[]{:S(2)}) async-start(), calls=%async_computation.2 | async-start | bytes 1179648 | tf_op jit(solution)/shard_map/all_gather | solution.py:19
  7.9 75.5 %all-gather.4.cloned.1.call-start = ((), (), s32[]{:S(2)}) async-start(), calls=%async_computation.1 | async-start | bytes 2621440 | tf_op jit(solution)/shard_map/all_gather | solution.py:18
  10.2 110.6 %all-gather.8.cloned.1.call-start = ((), (), s32[]{:S(2)}) async-start(), calls=%async_computation.3 | async-start | bytes 4718592 | tf_op jit(solution)/shard_map/all_gather | solution.py:23
  10.9 405.9 %reduce-scatter.2.cloned.1.call-start = ((), (), s32[]{:S(2)}) async-start(), calls=%async_computation.4 | async-start | bytes 20971520 | tf_op jit(solution)/shard_map/reduce_scatter | solution.py:43
  416.8 12.1 %copy-start.1 = (s32[2,4]{1,0:T(2,128)S(1)}, s32[2,4]{1,0:T(2,128)}, u32[]{:S(2)}) copy-start(s32[2,4]{1,0:T(2,128)} %param.7) | copy-start | bytes 100
Sparse Core Ops, SparseCore 0:
  9.9 25.0 all-gather.5
  37.1 46.1 all-gather.3
  85.8 34.9 all-gather.7
  136.9 279.8 reduce-scatter.1
where the time goes:
time: 437 us; the launch traced here: 435 us
  waiting for transfers between devices  381 us (87%)
  local copies, waits for them, and re-layouts  15.9 us (4%)
  other arithmetic  14 us (3%)
  between operations  13.8 us (3%)
  matrix products  10.6 us (2%)
    reduce_scatter x1, waiting for transfers between devices, local(): lax.psum_scatter(jnp.concatenate(pieces, axis=1), 'row', scatter_dimensio...  273 us
    all_gather x1, waiting for transfers between devices, local(): column = lax.all_gather(lhat_local, 'row', axis=0, tiled=True)  48.4 us
    all_gather x1, waiting for transfers between devices, local(): rows_all = lax.all_gather(lhat_local, 'col', axis=1, tiled=True)  33.7 us
    all_gather x1, waiting for transfers between devices, local(): sigma_rows = lax.all_gather(ancestor_inv, 'col', axis=1, tiled=True)  24 us
    unnamed x10, local copies, waits for them, and re-layouts  13.3 us
  transfers between devices with their start and end apart: 4, of which 4 were waited for; matrix products, arithmetic and copies ran while one was open for 3% of the time, Pallas kernels for 0%

commit v1 on v0

--- a/solution.py
+++ b/solution.py
@@ -1,10 +1,17 @@
+import functools
+
 import jax
 import jax.numpy as jnp
 from jax import lax
+from jax.experimental import pallas as pl
+from jax.experimental.pallas import tpu as pltpu
 from jax.sharding import PartitionSpec as P
 
 B = 256
 NS = 2
+NR = 4
+NC = 8
+MESH = pl.DeviceIdType.MESH
 
 
 def local(factor_panel, ancestor_inv, diag_inverse, structure):
@@ -47,10 +54,245 @@
     return (inverse_panel, diag_sigma)
 
 
+def kernel(structure, factor, anc, diag_in, panel_out, diag_out,
+           lt, pr, asl, a_hi, a_lo, q_hi, q_lo, diag_v,
+           zl_send, zl_recv, za_send, za_recv, ra_send, ra_recv, sa_send, sa_recv,
+           pc_send, pc_recv, ps_send, ps_recv, lc_sem, di_sem, do_sem):
+    r = lax.axis_index("row")
+    c = lax.axis_index("col")
+    wide = factor.shape[1] // NS
+    rows = factor.shape[0]
+    acols = anc.shape[1]
+    core = lax.rem(c, 2)
+    pos = c // 2
+    step = 1 - 2 * core
+
+    def ring_of(p):
+        y = p // 2
+        return 2 * y + lax.rem(lax.rem(p, 2) + y, 2)
+
+    def pos_of(q):
+        y = q // 2
+        return 2 * y + lax.rem(lax.rem(q, 2) + y, 2)
+
+    q_me = ring_of(pos)
+    q_src = ring_of(r)
+    hop = lax.rem((q_me - q_src) * step + 8, 4)
+
+    def ring_col(k):
+        return pos_of(lax.rem(q_me + k * step + 8, 4)) * 2 + core
+
+    nxt, prv = ring_col(1), ring_col(-1)
+    sib = pos * 2 + 1 - core
+    peers = [(lax.rem(r + d, NR), c) for d in range(1, NR)]
+
+    barrier = pltpu.get_barrier_semaphore()
+    for dev in peers + [(r, nxt), (r, prv), (r, sib)]:
+        pl.semaphore_signal(barrier, inc=1, device_id=dev, device_id_type=MESH)
+
+    diag_load = pltpu.make_async_copy(diag_in, diag_v, di_sem)
+    diag_load.start()
+    asl[c, r] = anc[...]
+    for s in range(NS):
+        part = factor[:, s * wide:(s + 1) * wide]
+        kept = jnp.where(structure[s, r] == 1, part.astype(jnp.float32), 0.0)
+        lt[r, s] = kept.T.astype(jnp.bfloat16)
+    pl.semaphore_wait(barrier, 6)
+
+    def remote(src, dst, send, recv, dev):
+        return pltpu.make_async_remote_copy(
+            src_ref=src, dst_ref=dst, send_sem=send, recv_sem=recv,
+            device_id=dev, device_id_type=MESH)
+
+    sends = []
+
+    def go(*args):
+        copy = remote(*args)
+        copy.start()
+        sends.append(copy)
+
+    for d in range(NR - 1):
+        go(asl.at[c, r], asl.at[c, r], za_send.at[d], za_recv.at[r], peers[d])
+    for s in range(NS):
+        for d in range(NR - 1):
+            go(lt.at[r, s], lt.at[r, s], zl_send.at[d, s], zl_recv.at[r, s], peers[d])
+
+    turn = 1 - 2 * (r // 2)
+
+    def chain_copy(z, t, s):
+        return remote(pr.at[core, z, s], pr.at[core, z, s], pc_send.at[t, s], pc_recv.at[t, s], (r, nxt))
+
+    def sib_copy(z, t, s):
+        return remote(pr.at[core, z, s], pr.at[core, z, s], ps_send.at[t, s], ps_recv.at[t, s], (r, sib))
+
+    def wait_lt(t, s):
+        z = lax.rem(r + t * turn + 8, NR)
+        remote(lt.at[z, s], lt.at[z, s], zl_send.at[0, s], zl_recv.at[z, s], peers[0]).wait_recv()
+
+    def chain(t):
+        z = lax.rem(r + t * turn + 8, NR)
+        for s in range(NS):
+            if t > 0:
+                wait_lt(t, s)
+
+            @pl.when(hop == 0)
+            def _():
+                copy = pltpu.make_async_copy(lt.at[z, s], pr.at[core, z, s], lc_sem.at[t, s])
+                copy.start()
+                copy.wait()
+
+            @pl.when(hop > 0)
+            def _():
+                chain_copy(z, t, s).wait_recv()
+
+            @pl.when(hop < 3)
+            def _():
+                chain_copy(z, t, s).start()
+
+            sib_copy(z, t, s).start()
+
+    def slab(k):
+        return ring_col(-k)
+
+    def ring(k):
+        col = slab(k)
+        if k == 0:
+            for d in range(1, NR):
+                z = lax.rem(r + d, NR)
+                remote(asl.at[c, z], asl.at[c, z], za_send.at[0], za_recv.at[z], peers[0]).wait_recv()
+        else:
+            remote(asl.at[col], asl.at[col], ra_send.at[k - 1], ra_recv.at[k - 1], (r, nxt)).wait_recv()
+        if k < 3:
+            go(asl.at[col], asl.at[col], ra_send.at[k], ra_recv.at[k], (r, nxt))
+        go(asl.at[col], asl.at[col], sa_send.at[k], sa_recv.at[k], (r, sib))
+
+    def split(col):
+        for z in range(NR):
+            a = asl[col, z]
+            hi = a.astype(jnp.bfloat16)
+            a_hi[col, z] = hi
+            a_lo[col, z] = (a - hi.astype(jnp.float32)).astype(jnp.bfloat16)
+
+    chain(0)
+    ring(0)
+    chain(1)
+    ring(1)
+    ring(2)
+    chain(2)
+    ring(3)
+    for k in range(4):
+        other = pos_of(lax.rem(q_me + k * step + 8, 4)) * 2 + 1 - core
+        remote(asl.at[other], asl.at[other], sa_send.at[k], sa_recv.at[k], (r, sib)).wait_recv()
+
+    @pl.loop(0, NC)
+    def _(col):
+        split(col)
+
+    chain(3)
+
+    def dot(a, b, dims):
+        return lax.dot_general(a, b, (dims, ((), ())), preferred_element_type=jnp.float32)
+
+    @pl.loop(0, NS * NR)
+    def _(it):
+        s = it // NR
+        z = lax.rem(it, NR)
+        rhs = jnp.concatenate([lt[b, s] for b in range(NR)], axis=1)
+        hi = jnp.concatenate([a_hi[col, z] for col in range(NC)], axis=1)
+        lo = jnp.concatenate([a_lo[col, z] for col in range(NC)], axis=1)
+        total = dot(hi, rhs, ((1,), (1,))) + dot(lo, rhs, ((1,), (1,)))
+        total = jnp.where(structure[s, z] == 1, -total, 0.0)
+        top = total.astype(jnp.bfloat16)
+        q_hi[s, z] = top
+        q_lo[s, z] = (total - top.astype(jnp.float32)).astype(jnp.bfloat16)
+        for m in range(NS):
+            @pl.when((z == r) & (s == m))
+            def _():
+                panel_out[:, m * wide:(m + 1) * wide] = total
+
+    for t in range(NR):
+        z = lax.rem(r + t * turn + 8, NR)
+        for s in range(NS):
+            remote(pr.at[1 - core, z, s], pr.at[1 - core, z, s], ps_send.at[t, s], ps_recv.at[t, s],
+                   (r, sib)).wait_recv()
+    diag_load.wait()
+
+    half = wide // 2
+
+    for k in range(2):
+        @pl.loop(0, 2)
+        def _(h):
+            for s in range(NS):
+                off = pl.multiple_of(h * half, half)
+                lhs = jnp.concatenate([pr[k, z, s, pl.ds(off, half), :] for z in range(NR)], axis=1)
+                hi = jnp.concatenate([q_hi[s, z] for z in range(NR)], axis=0)
+                lo = jnp.concatenate([q_lo[s, z] for z in range(NR)], axis=0)
+                total = dot(lhs, hi, ((1,), (0,))) + dot(lhs, lo, ((1,), (0,)))
+                where = pl.ds(pl.multiple_of(k * wide + h * half, half), half)
+                diag_v[where, s * wide:(s + 1) * wide] = diag_v[where, s * wide:(s + 1) * wide] - total
+        block = pl.ds(k * wide, wide)
+        pltpu.make_async_copy(diag_v.at[block], diag_out.at[block], do_sem.at[k]).start()
+
+    for copy in sends:
+        copy.wait_send()
+    for t in range(NR):
+        z = lax.rem(r + t * turn + 8, NR)
+        for s in range(NS):
+            @pl.when(hop < 3)
+            def _():
+                chain_copy(z, t, s).wait_send()
+
+            sib_copy(z, t, s).wait_send()
+    for k in range(2):
+        block = pl.ds(k * wide, wide)
+        pltpu.make_async_copy(diag_v.at[block], diag_out.at[block], do_sem.at[k]).wait()
+
+
+def local_kernel(factor_panel, ancestor_inv, diag_inverse, structure):
+    rows, width = factor_panel.shape
+    wide = width // NS
+    acols = ancestor_inv.shape[1]
+    dma = pltpu.SemaphoreType.DMA
+    bf16, f32 = jnp.bfloat16, jnp.float32
+    vmem = pl.BlockSpec(memory_space=pltpu.VMEM)
+    return pl.pallas_call(
+        kernel,
+        out_shape=(
+            jax.ShapeDtypeStruct((rows, width), f32),
+            jax.ShapeDtypeStruct(diag_inverse.shape, f32),
+        ),
+        in_specs=[pl.BlockSpec(memory_space=pltpu.SMEM), vmem, vmem, pl.BlockSpec(memory_space=pl.ANY)],
+        out_specs=(vmem, pl.BlockSpec(memory_space=pl.ANY)),
+        scratch_shapes=[
+            pltpu.VMEM((NR, NS, wide, rows), bf16),
+            pltpu.VMEM((2, NR, NS, wide, rows), bf16),
+            pltpu.VMEM((NC, NR, rows, acols), f32),
+            pltpu.VMEM((NC, NR, rows, acols), bf16),
+            pltpu.VMEM((NC, NR, rows, acols), bf16),
+            pltpu.VMEM((NS, NR, rows, wide), bf16),
+            pltpu.VMEM((NS, NR, rows, wide), bf16),
+            pltpu.VMEM(diag_inverse.shape, f32),
+            dma((NR - 1, NS)), dma((NR, NS)), dma((NR - 1,)), dma((NR,)),
+            dma((3,)), dma((3,)), dma((4,)), dma((4,)),
+            dma((NR, NS)), dma((NR, NS)), dma((NR, NS)), dma((NR, NS)),
+            dma((NR, NS)), dma, dma((2,)),
+        ],
+        compiler_params=pltpu.CompilerParams(
+            collective_id=0, has_side_effects=True, vmem_limit_bytes=48 << 20),
+    )(structure, factor_panel, ancestor_inv, diag_inverse)
+
+
 def solution(mesh):
     placed = (P("row", "col"), P("row", "col"), P("row", "col"), P())
+
+    def body(factor_panel, ancestor_inv, diag_inverse, structure):
+        rows, width = factor_panel.shape
+        fits = (mesh.shape["row"], mesh.shape["col"]) == (NR, NC) and rows == B
+        fits = fits and diag_inverse.shape[0] * NS == 2 * width
+        return (local_kernel if fits else local)(factor_panel, ancestor_inv, diag_inverse, structure)
+
     return jax.shard_map(
-        local,
+        body,
         mesh=mesh,
         in_specs=placed,
         out_specs=(P("row", "col"), P("row", "col")),

time: 437 us -> 142 us (0.32)
  the two profiles are of different devices: /device:TPU:5 before, /device:TPU:15 now
where the time goes in v1:
time: 142 us
  Pallas kernels  136 us (96%)
  local copies, waits for them, and re-layouts  5.6 us (4%)
    pallas_call x1, Pallas kernels, local_kernel(): pl.pallas_call(kernel, out_shape=(jax.ShapeDtypeStruct((rows, width), f32...  136 us
    unnamed x8, local copies, waits for them, and re-layouts  5.6 us

profile of v1, /device:TPU:15, one launch (start us, length us, event | category | flops | bytes accessed | tf_op | source)
XLA Modules:
  0.0 142.0 jit_solution(14956263172472140876)
XLA Ops:
  0.6 0.0 copy-start
  0.6 1.0 copy-done
  1.7 0.0 copy-start.1
  1.7 0.9 copy-done.1
  2.6 0.0 copy-start.2
  2.6 0.7 copy-done.2
  3.3 135.8 %shard_map.59 = (f32[256,1024]{1,0:T(8,128)S(1)}, f32[1024,1024]{1,0:T(8,128)S(1)}) custom-call(s32[2,4]{1,0:T(2,128)S(1)} %copy-done.2, bf16[256,1024]{1,0:T(8,128)(2,1)S(1)} %copy-done, f32[256,128]{1,0:T(8,128)S(1)} %copy-done.1, f32[1024,1024]{1,0:T(8,128)} %diag_in.1), custom_call_target="tpu_custom_call" | custom-call | tf_op jit(solution)/shard_map/pallas_call | solution.py:258
  139.0 1.0 copy.8
  140.0 2.0 %copy.9 = f32[1024,1024]{1,0:T(8,128)} copy(f32[1024,1024]{1,0:T(8,128)S(1)} %get-tuple-element.5) | data formatting | bytes 8388608
Async XLA Ops:
  0.6 1.0 copy-start
  1.7 0.9 copy-start.1
  2.6 0.7 copy-start.2

commit v2 on v0

--- a/solution.py
+++ b/solution.py
@@ -1,10 +1,17 @@
+import functools
+
 import jax
 import jax.numpy as jnp
 from jax import lax
+from jax.experimental import pallas as pl
+from jax.experimental.pallas import tpu as pltpu
 from jax.sharding import PartitionSpec as P
 
 B = 256
 NS = 2
+NR = 4
+NC = 8
+MESH = pl.DeviceIdType.MESH
 
 
 def local(factor_panel, ancestor_inv, diag_inverse, structure):
@@ -47,10 +54,317 @@
     return (inverse_panel, diag_sigma)
 
 
+def kernel(structure, factor, anc, diag_in, panel_out, diag_out,
+           lt, pr, asl, a_hi, a_lo, q_hi, q_lo,
+           zl_send, zl_recv, za_send, za_recv, ra_send, ra_recv, sa_send, sa_recv,
+           pc_send, pc_recv, ps_send, ps_recv, lc_sem, di_sem):
+    r = lax.axis_index("row")
+    c = lax.axis_index("col")
+    wide = factor.shape[1] // NS
+    core = lax.rem(c, 2)
+    pos = c // 2
+    step = 1 - 2 * core
+
+    def gray(p):
+        y = p // 2
+        return 2 * y + lax.rem(lax.rem(p, 2) + y, 2)
+
+    q_me = gray(pos)
+    hop = lax.rem((q_me - gray(r)) * step + 8, 4)
+
+    def ring_col(k, kind):
+        return gray(lax.rem(q_me + k * step + 8, 4)) * 2 + kind
+
+    nxt, prv = ring_col(1, core), ring_col(-1, core)
+    sib = pos * 2 + 1 - core
+    has = (r < NR - 1, r > 0)
+    to = ((lax.rem(r + 1, NR), c), (lax.rem(r + NR - 1, NR), c))
+    order = [r, r + 1 - 2 * (r // 3), lax.rem(r + 2, 3) - r // 3, 3 * (1 - r // 2)]
+
+    barrier = pltpu.get_barrier_semaphore()
+    for dev in ((r, nxt), (r, prv), (r, sib)) + to:
+        pl.semaphore_signal(barrier, inc=1, device_id=dev, device_id_type=MESH)
+
+    diag_load = pltpu.make_async_copy(diag_in, diag_out, di_sem)
+    diag_load.start()
+    asl[c, r] = anc[...]
+    for s in range(NS):
+        part = factor[:, s * wide:(s + 1) * wide]
+        kept = jnp.where(structure[s, r] == 1, part.astype(jnp.float32), 0.0)
+        lt[r, s] = kept.T.astype(jnp.bfloat16)
+    pl.semaphore_wait(barrier, 5)
+
+    def remote(ref, send, recv, dev, src=None):
+        return pltpu.make_async_remote_copy(
+            src_ref=ref if src is None else src, dst_ref=ref, send_sem=send, recv_sem=recv,
+            device_id=dev, device_id_type=MESH)
+
+    sends = []
+
+    def go(cond, copy):
+        sends.append((cond, copy))
+        if cond is None:
+            copy.start()
+        else:
+            @pl.when(cond)
+            def _():
+                copy.start()
+
+    def row_send(j, s=None):
+        for way in range(2):
+            z = (r - j) if way == 0 else (r + j)
+            there = (z >= 0) & (z < NR) & has[way]
+            z = lax.rem(z + NR, NR)
+            if s is None:
+                copy = remote(asl.at[c, z], za_send.at[way, j], za_recv.at[way, j], to[way])
+            else:
+                copy = remote(lt.at[z, s], zl_send.at[way, j, s], zl_recv.at[way, j, s], to[way])
+            go(there, copy)
+
+    def row_wait(j, s=None):
+        for way in range(2):
+            z = (r - 1 - j) if way == 0 else (r + 1 + j)
+            there = (z >= 0) & (z < NR)
+            z = lax.rem(z + NR, NR)
+
+            @pl.when(there)
+            def _():
+                if s is None:
+                    remote(asl.at[c, z], za_send.at[way, j], za_recv.at[way, j], to[way]).wait_recv()
+                else:
+                    remote(lt.at[z, s], zl_send.at[way, j, s], zl_recv.at[way, j, s], to[way]).wait_recv()
+
+    def chain_copy(t, s, src=None):
+        return remote(pr.at[core, order[t], s], pc_send.at[t, s], pc_recv.at[t, s], (r, nxt), src)
+
+    def sib_copy(t, s, src=None):
+        return remote(pr.at[core, order[t], s], ps_send.at[t, s], ps_recv.at[t, s], (r, sib), src)
+
+    def own_copy(t, s):
+        z = order[t]
+        return pltpu.make_async_copy(lt.at[z, s], pr.at[core, z, s], lc_sem.at[t, s])
+
+    def chain(t, s, low, high):
+        if low == 0:
+            @pl.when(hop == 0)
+            def _():
+                src = lt.at[order[t], s]
+                chain_copy(t, s, src).start()
+                sib_copy(t, s, src).start()
+                own_copy(t, s).start()
+
+        if high > 0:
+            @pl.when((hop >= max(low, 1)) & (hop <= high))
+            def _():
+                chain_copy(t, s).wait_recv()
+
+                @pl.when(hop < 3)
+                def _():
+                    chain_copy(t, s).start()
+
+                sib_copy(t, s).start()
+
+    def ring(t, k):
+        part = asl.at[ring_col(-k, core), order[t]]
+        if k > 0:
+            remote(part, ra_send.at[t, k - 1], ra_recv.at[t, k - 1], (r, nxt)).wait_recv()
+        if k < 3:
+            go(None, remote(part, ra_send.at[t, k], ra_recv.at[t, k], (r, nxt)))
+        go(None, remote(part, sa_send.at[t, k], sa_recv.at[t, k], (r, sib)))
+
+    row_send(0)
+    chain(0, 0, 0, 0)
+    ring(0, 0)
+    row_wait(0)
+    row_send(1)
+    row_send(0, 0)
+    ring(1, 0)
+    chain(0, 0, 1, 1)
+    chain(0, 1, 0, 0)
+    ring(0, 1)
+    row_wait(1)
+    row_send(2)
+    row_send(0, 1)
+    ring(2, 0)
+    ring(0, 2)
+    ring(1, 1)
+    chain(0, 0, 2, 2)
+    chain(0, 1, 1, 1)
+    ring(0, 3)
+    ring(1, 2)
+    chain(0, 0, 3, 3)
+    row_wait(0, 0)
+    row_send(1, 0)
+    chain(1, 0, 0, 0)
+    chain(0, 1, 2, 2)
+    ring(2, 1)
+    ring(1, 3)
+    row_wait(2)
+    ring(3, 0)
+    ring(2, 2)
+    chain(1, 0, 1, 1)
+    chain(0, 1, 3, 3)
+    row_wait(0, 1)
+    row_send(1, 1)
+    chain(1, 1, 0, 0)
+    chain(1, 0, 2, 2)
+    ring(3, 1)
+    ring(2, 3)
+    row_wait(1, 0)
+    row_send(2, 0)
+    chain(2, 0, 0, 0)
+    chain(1, 1, 1, 1)
+    chain(1, 0, 3, 3)
+    ring(3, 2)
+    chain(2, 0, 1, 1)
+    chain(1, 1, 2, 2)
+    row_wait(1, 1)
+    row_send(2, 1)
+    chain(2, 1, 0, 0)
+    ring(3, 3)
+    chain(1, 1, 3, 3)
+    chain(2, 0, 2, 2)
+    for t in range(NR):
+        for k in range(4):
+            other = asl.at[ring_col(k, 1 - core), order[t]]
+            remote(other, sa_send.at[t, k], sa_recv.at[t, k], (r, sib)).wait_recv()
+
+    @pl.loop(0, NC)
+    def _(col):
+        for z in range(NR):
+            a = asl[col, z]
+            hi = a.astype(jnp.bfloat16)
+            a_hi[col, z] = hi
+            a_lo[col, z] = (a - hi.astype(jnp.float32)).astype(jnp.bfloat16)
+
+    chain(2, 1, 1, 1)
+    chain(2, 0, 3, 3)
+
+    def dot(a, b, dims):
+        return lax.dot_general(a, b, (dims, ((), ())), preferred_element_type=jnp.float32)
+
+    def panel(s):
+        @pl.loop(0, NR)
+        def _(z):
+            rhs = jnp.concatenate([lt[b, s] for b in range(NR)], axis=1)
+            hi = jnp.concatenate([a_hi[col, z] for col in range(NC)], axis=1)
+            lo = jnp.concatenate([a_lo[col, z] for col in range(NC)], axis=1)
+            total = dot(hi, rhs, ((1,), (1,))) + dot(lo, rhs, ((1,), (1,)))
+            total = jnp.where(structure[s, z] == 1, -total, 0.0)
+            top = total.astype(jnp.bfloat16)
+            q_hi[s, z] = top
+            q_lo[s, z] = (total - top.astype(jnp.float32)).astype(jnp.bfloat16)
+
+            @pl.when(z == r)
+            def _():
+                panel_out[:, s * wide:(s + 1) * wide] = total
+
+    def arrived(t, s):
+        @pl.when(hop == 0)
+        def _():
+            own_copy(t, s).wait()
+
+        remote(pr.at[1 - core, order[t], s], ps_send.at[t, s], ps_recv.at[t, s], (r, sib)).wait_recv()
+
+    half = wide // 2
+
+    def update(s, ts, first=0, last=4):
+        @pl.loop(first, last)
+        def _(it):
+            k = it // 2
+            off = pl.multiple_of((it - 2 * k) * half, half)
+            where = pl.ds(pl.multiple_of(it * half, half), half)
+            lhs = jnp.concatenate([pr[k, order[t], s, pl.ds(off, half), :] for t in ts], axis=1)
+            hi = jnp.concatenate([q_hi[s, order[t]] for t in ts], axis=0)
+            lo = jnp.concatenate([q_lo[s, order[t]] for t in ts], axis=0)
+            total = dot(lhs, hi, ((1,), (0,))) + dot(lhs, lo, ((1,), (0,)))
+            here = slice(s * wide, (s + 1) * wide)
+            diag_out[where, here] = diag_out[where, here] - total
+
+    row_wait(2, 0)
+    chain(3, 0, 0, 0)
+    chain(2, 1, 2, 2)
+    panel(0)
+    chain(3, 0, 1, 1)
+    chain(2, 1, 3, 3)
+    chain(3, 0, 2, 2)
+    row_wait(2, 1)
+    chain(3, 1, 0, 0)
+    diag_load.wait()
+    panel(1)
+    chain(3, 1, 1, 1)
+    chain(3, 0, 3, 3)
+    for t in range(NR):
+        arrived(t, 0)
+    update(0, (0, 1, 2, 3), 0, 2)
+    chain(3, 1, 2, 2)
+    update(0, (0, 1, 2, 3), 2, 4)
+    for t in range(3):
+        arrived(t, 1)
+    update(1, (0, 1, 2), 0, 2)
+    chain(3, 1, 3, 3)
+    update(1, (0, 1, 2), 2, 4)
+    arrived(3, 1)
+    update(1, (3,))
+
+    for cond, copy in sends:
+        if cond is None:
+            copy.wait_send()
+        else:
+            pl.when(cond)(copy.wait_send)
+    for t in range(NR):
+        for s in range(NS):
+            @pl.when(hop < 3)
+            def _():
+                chain_copy(t, s).wait_send()
+
+            sib_copy(t, s).wait_send()
+
+
+def local_kernel(factor_panel, ancestor_inv, diag_inverse, structure):
+    rows, width = factor_panel.shape
+    wide = width // NS
+    acols = ancestor_inv.shape[1]
+    dma = pltpu.SemaphoreType.DMA
+    bf16, f32 = jnp.bfloat16, jnp.float32
+    vmem = pl.BlockSpec(memory_space=pltpu.VMEM)
+    return pl.pallas_call(
+        kernel,
+        out_shape=(
+            jax.ShapeDtypeStruct((rows, width), f32),
+            jax.ShapeDtypeStruct(diag_inverse.shape, f32),
+        ),
+        in_specs=[pl.BlockSpec(memory_space=pltpu.SMEM), vmem, vmem, pl.BlockSpec(memory_space=pl.ANY)],
+        out_specs=(vmem, vmem),
+        scratch_shapes=[
+            pltpu.VMEM((NR, NS, wide, rows), bf16),
+            pltpu.VMEM((2, NR, NS, wide, rows), bf16),
+            pltpu.VMEM((NC, NR, rows, acols), f32),
+            pltpu.VMEM((NC, NR, rows, acols), bf16),
+            pltpu.VMEM((NC, NR, rows, acols), bf16),
+            pltpu.VMEM((NS, NR, rows, wide), bf16),
+            pltpu.VMEM((NS, NR, rows, wide), bf16),
+            dma((2, NR - 1, NS)), dma((2, NR - 1, NS)), dma((2, NR - 1)), dma((2, NR - 1)),
+            dma((NR, 3)), dma((NR, 3)), dma((NR, 4)), dma((NR, 4)),
+            dma((NR, NS)), dma((NR, NS)), dma((NR, NS)), dma((NR, NS)),
+            dma((NR, NS)), dma,
+        ],
+        compiler_params=pltpu.CompilerParams(
+            collective_id=0, has_side_effects=True, vmem_limit_bytes=48 << 20),
+    )(structure, factor_panel, ancestor_inv, diag_inverse)
+
+
 def solution(mesh):
     placed = (P("row", "col"), P("row", "col"), P("row", "col"), P())
+
+    def body(factor_panel, ancestor_inv, diag_inverse, structure):
+        rows, width = factor_panel.shape
+        fits = (mesh.shape["row"], mesh.shape["col"]) == (NR, NC) and rows == B
+        fits = fits and diag_inverse.shape[0] * NS == 2 * width
+        return (local_kernel if fits else local)(factor_panel, ancestor_inv, diag_inverse, structure)
+
     return jax.shard_map(
-        local,
+        body,
         mesh=mesh,
         in_specs=placed,
         out_specs=(P("row", "col"), P("row", "col")),

time: 437 us -> 79.2 us (0.18)
  waiting for transfers between devices: 381 us -> 0 us
  Pallas kernels: 0 us -> 72.8 us
  other arithmetic: 14 us -> 0 us
  between operations: 13.8 us -> 0.65 us
  matrix products: 10.6 us -> 0 us
  local copies, waits for them, and re-layouts: 15.9 us -> 5.6 us
    reduce_scatter x1 -> x0, waiting for transfers between devices: 273 us -> none  [local(): lax.psum_scatter(jnp.concatenate(pieces, axis=1), 'row', scatter_dimensio...]
    all_gather x3 -> x0, waiting for transfers between devices: 106 us -> none  [the longest x1 48.4 us: local(): column = lax.all_gather(lhat_local, 'row', axis=0, tiled=True)]
    pallas_call x0 -> x1, Pallas kernels: none -> 72.8 us  [local_kernel(): pl.pallas_call(kernel, out_shape=(jax.ShapeDtypeStruct((rows, width), f32...]
    dot_general x3 -> x0, matrix products: 10.6 us -> none  [the longest x2 6.92 us: local(): lax.dot_general(window, target, (((0,), (0,)), ((), ())), precision=lax.P...]
    unnamed x10 -> x8, local copies, waits for them, and re-layouts: 13.3 us -> 5.6 us
    sub x1 -> x0, other arithmetic: 6.79 us -> none  [local(): diag_sigma = diag_inverse - update]
    concatenate x1 -> x0, other arithmetic: 6.38 us -> none  [local(): jnp.concatenate(pieces, axis=1)]
  transfers between devices with their start and end apart: 4 -> 0, of which waited for: 4 -> 0; matrix products, arithmetic and copies ran while one was open for 3% -> 0% of each run, Pallas kernels for 0% -> 0%
where the time goes in v2:
time: 79.2 us; the launch traced here: 79 us
  Pallas kernels  72.8 us (92%)
  local copies, waits for them, and re-layouts  5.6 us (7%)
    pallas_call x1, Pallas kernels, local_kernel(): pl.pallas_call(kernel, out_shape=(jax.ShapeDtypeStruct((rows, width), f32...  72.8 us
    unnamed x8, local copies, waits for them, and re-layouts  5.6 us

profile of v2, /device:TPU:5, one launch (start us, length us, event | category | flops | bytes accessed | tf_op | source)
XLA Modules:
  0.0 79.0 jit_solution(1100760984914960853)
XLA Ops:
  0.6 0.0 copy-start
  0.6 1.0 %copy-done = bf16[256,1024]{1,0:T(8,128)(2,1)S(1)} copy-done((bf16[256,1024]{1,0:T(8,128)(2,1)S(1)}, bf16[256,1024]{1,0:T(8,128)(2,1)}, u32[]{:S(2)}) %copy-start) | copy-done | bytes 524312
  1.7 0.0 copy-start.1
  1.7 0.9 %copy-done.1 = f32[256,128]{1,0:T(8,128)S(1)} copy-done((f32[256,128]{1,0:T(8,128)S(1)}, f32[256,128]{1,0:T(8,128)}, u32[]{:S(2)}) %copy-start.1) | copy-done | bytes 131096
  2.6 0.0 copy-start.2
  2.6 0.7 copy-done.2
  3.3 72.8 %shard_map.59 = (f32[256,1024]{1,0:T(8,128)S(1)}, f32[1024,1024]{1,0:T(8,128)S(1)}) custom-call(s32[2,4]{1,0:T(2,128)S(1)} %copy-done.2, bf16[256,1024]{1,0:T(8,128)(2,1)S(1)} %copy-done, f32[256,128]{1,0:T(8,128)S(1)} %copy-done.1, f32[1024,1024]{1,0:T(8,128)} %diag_in.1), custom_call_target="tpu_custom_call" | custom-call | tf_op jit(solution)/shard_map/pallas_call | solution.py:331
  76.0 1.0 %copy.8 = f32[256,1024]{1,0:T(8,128)} copy(f32[256,1024]{1,0:T(8,128)S(1)} %get-tuple-element.4) | data formatting | bytes 2097152
  77.0 2.0 %copy.9 = f32[1024,1024]{1,0:T(8,128)} copy(f32[1024,1024]{1,0:T(8,128)S(1)} %get-tuple-element.5) | data formatting | bytes 8388608
Async XLA Ops:
  0.6 1.0 %copy-start = (bf16[256,1024]{1,0:T(8,128)(2,1)S(1)}, bf16[256,1024]{1,0:T(8,128)(2,1)}, u32[]{:S(2)}) copy-start(bf16[256,1024]{1,0:T(8,128)(2,1)} %factor.1) | copy-start | bytes 1572868
  1.7 0.9 %copy-start.1 = (f32[256,128]{1,0:T(8,128)S(1)}, f32[256,128]{1,0:T(8,128)}, u32[]{:S(2)}) copy-start(f32[256,128]{1,0:T(8,128)} %anc.1) | copy-start | bytes 393220
  2.6 0.7 copy-start.2

commit v3 on v2

--- a/solution.py
+++ b/solution.py
@@ -11,6 +11,7 @@
 NS = 2
 NR = 4
 NC = 8
+SUB = 4
 MESH = pl.DeviceIdType.MESH
 
 
@@ -55,7 +56,7 @@
 
 
 def kernel(structure, factor, anc, diag_in, panel_out, diag_out,
-           lt, pr, asl, a_hi, a_lo, q_hi, q_lo,
+           lt, pr, asl, a_hi, a_lo, q_sum, q_hi, q_lo,
            zl_send, zl_recv, za_send, za_recv, ra_send, ra_recv, sa_send, sa_recv,
            pc_send, pc_recv, ps_send, ps_recv, lc_sem, di_sem):
     r = lax.axis_index("row")
@@ -134,11 +135,15 @@
                 else:
                     remote(lt.at[z, s], zl_send.at[way, j, s], zl_recv.at[way, j, s], to[way]).wait_recv()
 
-    def chain_copy(t, s, src=None):
-        return remote(pr.at[core, order[t], s], pc_send.at[t, s], pc_recv.at[t, s], (r, nxt), src)
-
-    def sib_copy(t, s, src=None):
-        return remote(pr.at[core, order[t], s], ps_send.at[t, s], ps_recv.at[t, s], (r, sib), src)
+    def parts(t):
+        count = SUB if t == NR - 1 else 1
+        return [(i, pl.ds(i * (wide // count), wide // count)) for i in range(count)]
+
+    def chain_copy(t, s, i, cut, src=None):
+        return remote(pr.at[core, order[t], s, cut], pc_send.at[t, s, i], pc_recv.at[t, s, i], (r, nxt), src)
+
+    def sib_copy(t, s, i, cut, src=None):
+        return remote(pr.at[core, order[t], s, cut], ps_send.at[t, s, i], ps_recv.at[t, s, i], (r, sib), src)
 
     def own_copy(t, s):
         z = order[t]
@@ -148,21 +153,23 @@
         if low == 0:
             @pl.when(hop == 0)
             def _():
-                src = lt.at[order[t], s]
-                chain_copy(t, s, src).start()
-                sib_copy(t, s, src).start()
+                for i, cut in parts(t):
+                    src = lt.at[order[t], s, cut]
+                    chain_copy(t, s, i, cut, src).start()
+                    sib_copy(t, s, i, cut, src).start()
                 own_copy(t, s).start()
 
         if high > 0:
             @pl.when((hop >= max(low, 1)) & (hop <= high))
             def _():
-                chain_copy(t, s).wait_recv()
-
-                @pl.when(hop < 3)
-                def _():
-                    chain_copy(t, s).start()
-
-                sib_copy(t, s).start()
+                for i, cut in parts(t):
+                    chain_copy(t, s, i, cut).wait_recv()
+
+                    @pl.when(hop < 3)
+                    def _():
+                        chain_copy(t, s, i, cut).start()
+
+                    sib_copy(t, s, i, cut).start()
 
     def ring(t, k):
         part = asl.at[ring_col(-k, core), order[t]]
@@ -171,6 +178,34 @@
         if k < 3:
             go(None, remote(part, ra_send.at[t, k], ra_recv.at[t, k], (r, nxt)))
         go(None, remote(part, sa_send.at[t, k], sa_recv.at[t, k], (r, sib)))
+
+    def dot(a, b, dims):
+        return lax.dot_general(a, b, (dims, ((), ())), preferred_element_type=jnp.float32)
+
+    def product(s, z, ts):
+        rhs = jnp.concatenate([lt[order[t], s] for t in ts], axis=1)
+        cols = [2 * order[t] + i for t in ts for i in range(2)]
+        hi = jnp.concatenate([a_hi[col, z] for col in cols], axis=1)
+        lo = jnp.concatenate([a_lo[col, z] for col in cols], axis=1)
+        return dot(hi, rhs, ((1,), (1,))) + dot(lo, rhs, ((1,), (1,)))
+
+    def panel_start(s):
+        @pl.loop(0, NR)
+        def _(z):
+            q_sum[s, z] = product(s, z, (0, 1, 2))
+
+    def panel_end(s):
+        @pl.loop(0, NR)
+        def _(z):
+            total = product(s, z, (0, 1, 2, 3))
+            total = jnp.where(structure[s, z] == 1, -total, 0.0)
+            top = total.astype(jnp.bfloat16)
+            q_hi[s, z] = top
+            q_lo[s, z] = (total - top.astype(jnp.float32)).astype(jnp.bfloat16)
+
+            @pl.when(z == r)
+            def _():
+                panel_out[:, s * wide:(s + 1) * wide] = total
 
     row_send(0)
     chain(0, 0, 0, 0)
@@ -239,32 +274,15 @@
 
     chain(2, 1, 1, 1)
     chain(2, 0, 3, 3)
-
-    def dot(a, b, dims):
-        return lax.dot_general(a, b, (dims, ((), ())), preferred_element_type=jnp.float32)
-
-    def panel(s):
-        @pl.loop(0, NR)
-        def _(z):
-            rhs = jnp.concatenate([lt[b, s] for b in range(NR)], axis=1)
-            hi = jnp.concatenate([a_hi[col, z] for col in range(NC)], axis=1)
-            lo = jnp.concatenate([a_lo[col, z] for col in range(NC)], axis=1)
-            total = dot(hi, rhs, ((1,), (1,))) + dot(lo, rhs, ((1,), (1,)))
-            total = jnp.where(structure[s, z] == 1, -total, 0.0)
-            top = total.astype(jnp.bfloat16)
-            q_hi[s, z] = top
-            q_lo[s, z] = (total - top.astype(jnp.float32)).astype(jnp.bfloat16)
-
-            @pl.when(z == r)
-            def _():
-                panel_out[:, s * wide:(s + 1) * wide] = total
+    chain(2, 1, 2, 2)
 
     def arrived(t, s):
         @pl.when(hop == 0)
         def _():
             own_copy(t, s).wait()
 
-        remote(pr.at[1 - core, order[t], s], ps_send.at[t, s], ps_recv.at[t, s], (r, sib)).wait_recv()
+        for i, cut in parts(t):
+            remote(pr.at[1 - core, order[t], s, cut], ps_send.at[t, s, i], ps_recv.at[t, s, i], (r, sib)).wait_recv()
 
     half = wide // 2
 
@@ -281,17 +299,16 @@
             here = slice(s * wide, (s + 1) * wide)
             diag_out[where, here] = diag_out[where, here] - total
 
+    diag_load.wait()
     row_wait(2, 0)
     chain(3, 0, 0, 0)
-    chain(2, 1, 2, 2)
-    panel(0)
+    chain(2, 1, 3, 3)
+    panel_end(0)
     chain(3, 0, 1, 1)
-    chain(2, 1, 3, 3)
-    chain(3, 0, 2, 2)
     row_wait(2, 1)
     chain(3, 1, 0, 0)
-    diag_load.wait()
-    panel(1)
+    chain(3, 0, 2, 2)
+    panel_end(1)
     chain(3, 1, 1, 1)
     chain(3, 0, 3, 3)
     for t in range(NR):
@@ -301,9 +318,8 @@
     update(0, (0, 1, 2, 3), 2, 4)
     for t in range(3):
         arrived(t, 1)
-    update(1, (0, 1, 2), 0, 2)
+    update(1, (0, 1, 2))
     chain(3, 1, 3, 3)
-    update(1, (0, 1, 2), 2, 4)
     arrived(3, 1)
     update(1, (3,))
 
@@ -314,11 +330,12 @@
             pl.when(cond)(copy.wait_send)
     for t in range(NR):
         for s in range(NS):
-            @pl.when(hop < 3)
-            def _():
-                chain_copy(t, s).wait_send()
-
-            sib_copy(t, s).wait_send()
+            for i, cut in parts(t):
+                @pl.when(hop < 3)
+                def _():
+                    chain_copy(t, s, i, cut).wait_send()
+
+                sib_copy(t, s, i, cut).wait_send()
 
 
 def local_kernel(factor_panel, ancestor_inv, diag_inverse, structure):
@@ -342,11 +359,12 @@
             pltpu.VMEM((NC, NR, rows, acols), f32),
             pltpu.VMEM((NC, NR, rows, acols), bf16),
             pltpu.VMEM((NC, NR, rows, acols), bf16),
+            pltpu.VMEM((NS, NR, rows, wide), f32),
             pltpu.VMEM((NS, NR, rows, wide), bf16),
             pltpu.VMEM((NS, NR, rows, wide), bf16),
             dma((2, NR - 1, NS)), dma((2, NR - 1, NS)), dma((2, NR - 1)), dma((2, NR - 1)),
             dma((NR, 3)), dma((NR, 3)), dma((NR, 4)), dma((NR, 4)),
-            dma((NR, NS)), dma((NR, NS)), dma((NR, NS)), dma((NR, NS)),
+            dma((NR, NS, SUB)), dma((NR, NS, SUB)), dma((NR, NS, SUB)), dma((NR, NS, SUB)),
             dma((NR, NS)), dma,
         ],
         compiler_params=pltpu.CompilerParams(

time: 79.2 us -> 79.4 us (level)
  no operation moved by 1% of the time
where the time goes in v3:
time: 79.4 us; the launch traced here: 79.2 us
  Pallas kernels  73 us (92%)
  local copies, waits for them, and re-layouts  5.6 us (7%)
    pallas_call x1, Pallas kernels, local_kernel(): pl.pallas_call(kernel, out_shape=(jax.ShapeDtypeStruct((rows, width), f32...  73 us
    unnamed x8, local copies, waits for them, and re-layouts  5.6 us

profile of v3, /device:TPU:5, one launch (start us, length us, event | category | flops | bytes accessed | tf_op | source)
XLA Modules:
  0.0 79.2 jit_solution(9680014361217488184)
XLA Ops:
  0.6 0.0 copy-start
  0.6 1.0 %copy-done = bf16[256,1024]{1,0:T(8,128)(2,1)S(1)} copy-done((bf16[256,1024]{1,0:T(8,128)(2,1)S(1)}, bf16[256,1024]{1,0:T(8,128)(2,1)}, u32[]{:S(2)}) %copy-start) | copy-done | bytes 524312
  1.7 0.0 copy-start.1
  1.7 0.9 %copy-done.1 = f32[256,128]{1,0:T(8,128)S(1)} copy-done((f32[256,128]{1,0:T(8,128)S(1)}, f32[256,128]{1,0:T(8,128)}, u32[]{:S(2)}) %copy-start.1) | copy-done | bytes 131096
  2.6 0.0 copy-start.2
  2.6 0.7 copy-done.2
  3.3 73.0 %shard_map.59 = (f32[256,1024]{1,0:T(8,128)S(1)}, f32[1024,1024]{1,0:T(8,128)S(1)}) custom-call(s32[2,4]{1,0:T(2,128)S(1)} %copy-done.2, bf16[256,1024]{1,0:T(8,128)(2,1)S(1)} %copy-done, f32[256,128]{1,0:T(8,128)S(1)} %copy-done.1, f32[1024,1024]{1,0:T(8,128)} %diag_in.1), custom_call_target="tpu_custom_call" | custom-call | tf_op jit(solution)/shard_map/pallas_call | solution.py:348
  76.2 1.0 %copy.8 = f32[256,1024]{1,0:T(8,128)} copy(f32[256,1024]{1,0:T(8,128)S(1)} %get-tuple-element.4) | data formatting | bytes 2097152
  77.2 2.0 %copy.9 = f32[1024,1024]{1,0:T(8,128)} copy(f32[1024,1024]{1,0:T(8,128)S(1)} %get-tuple-element.5) | data formatting | bytes 8388608
Async XLA Ops:
  0.6 1.0 %copy-start = (bf16[256,1024]{1,0:T(8,128)(2,1)S(1)}, bf16[256,1024]{1,0:T(8,128)(2,1)}, u32[]{:S(2)}) copy-start(bf16[256,1024]{1,0:T(8,128)(2,1)} %factor.1) | copy-start | bytes 1572868
  1.7 0.9 %copy-start.1 = (f32[256,128]{1,0:T(8,128)S(1)}, f32[256,128]{1,0:T(8,128)}, u32[]{:S(2)}) copy-start(f32[256,128]{1,0:T(8,128)} %anc.1) | copy-start | bytes 393220
  2.6 0.7 copy-start.2
